TPU v7x, 32 devices: a whole 2x2x4 slice. The times are simulated.
32 devices in a mesh: row: 4 (over y, x), col: 8 (over z, core).
Axes of the slice: x: 2, y: 2, z: 4, core: 2. Of those that a mesh axis runs over, the one named last changes fastest.
Arguments:
- omega: bfloat16 [16384, 16384], P('row', 'col'), may hold values from -0.36 to 2, as said below
- samples: bfloat16 [512, 16384], P(None, 'col'), may hold values from -6 to 6
- pair_tiles: int32 [320, 2], replicated, may hold values from 0 to 127, as said below
- step: float32 [1], replicated, may hold values from 0.5 to 1
- penalty: int32 [1], replicated, may hold values from 0 to 15
Outputs:
- new_upper: float32 [320, 128, 128], P(('row', 'col'))
- new_lower: float32 [320, 128, 128], P(('row', 'col'))
Inputs may be any that keep to these rules, and one draw needn't show every extreme that they name: `omega`: diagonal entries lie between 1 and 2; the others are small and dense. `pair_tiles`: each row is a tile pair (I, J) with I <= J; no owner lists a pair twice, and a pair may be listed by several owners. Rows k * 10 to (k + 1) * 10 - 1 belong to owner k, counted over row+col with row the slower. Taking as a row block the tile rows held by one index of row, each owner has exactly one pair for every pair of row blocks (block of I no later than block of J). Of the distinct tiles (I, J) and (J, I) of one owner at most one lies in the block of omega held by any one device.
All inputs are finite; a program needn't handle non-finite values.
Results may differ from a plain program's by a relative error of at most 0.0058.
Values may be sent and summed in bfloat16 or wider, within the bound.
No kernel may reach another device: no remote copies, remote signals or barrier semaphores. Data moves between devices by JAX's collectives and lax.ppermute only.
A program may use at most 128 MiB of HBM per device.

v0:
```python
import jax
import jax.numpy as jnp
from jax import lax
from jax.sharding import PartitionSpec as P

TILE = 128


def local(omega, samples, pair_tiles, step, penalty):
    col_count = lax.axis_size("col")
    row_index = lax.axis_index("row")
    col_index = lax.axis_index("col")
    device_count = lax.axis_size("row") * col_count
    own_index = row_index * col_count + col_index
    row_tiles = omega.shape[0] // TILE
    col_tiles = omega.shape[1] // TILE
    sample_count = samples.shape[0]
    partial_value = lax.dot_general(
        omega, samples, (((1,), (1,)), ((), ())), preferred_element_type=jnp.float32
    )
    shared = lax.psum_scatter(partial_value, "col", scatter_dimension=0, tiled=True).astype(
        jnp.bfloat16
    )
    product = lax.dot_general(
        samples,
        lax.all_gather(shared, "col", axis=0, tiled=True),
        (((0,), (1,)), ((), ())),
        preferred_element_type=jnp.float32,
    )
    moments = (product / sample_count).astype(jnp.bfloat16)
    pair_count = pair_tiles.shape[0] // device_count
    item_count = 2 * pair_count
    item_rows = jnp.stack([pair_tiles[:, 0], pair_tiles[:, 1]], axis=1).reshape(
        device_count, item_count
    )
    item_cols = jnp.stack([pair_tiles[:, 1], pair_tiles[:, 0]], axis=1).reshape(
        device_count, item_count
    )
    positions = jnp.arange(item_count)
    repeated = (positions % 2 == 1)[None, :] & (item_rows == item_cols)
    held = (
        (item_rows // row_tiles == row_index) & (item_cols // col_tiles == col_index) & ~repeated
    ).astype(jnp.int32)
    filled = jnp.sum(held, axis=1)
    local_rows = jnp.sum(held * (item_rows - row_index * row_tiles), axis=1)
    local_cols = jnp.sum(held * (item_cols - col_index * col_tiles), axis=1)
    moment_tiles = moments.reshape(col_tiles, TILE, row_tiles, TILE)[local_cols, :, local_rows, :]
    omega_tiles = omega.reshape(row_tiles, TILE, col_tiles, TILE)[local_rows, :, local_cols, :]
    keep = (filled > 0)[:, None, None]
    send_moments = jnp.where(keep, moment_tiles, jnp.zeros_like(moment_tiles))
    send_omega = jnp.where(keep, omega_tiles, jnp.zeros_like(omega_tiles))
    got_moments, got_omega = (
        lax.all_to_all(send_moments, ("row", "col"), split_axis=0, concat_axis=0, tiled=True),
        lax.all_to_all(send_omega, ("row", "col"), split_axis=0, concat_axis=0, tiled=True),
    )
    mine_rows = lax.dynamic_index_in_dim(item_rows, own_index, 0, keepdims=False)
    mine_cols = lax.dynamic_index_in_dim(item_cols, own_index, 0, keepdims=False)
    holder = mine_rows // row_tiles * col_count + mine_cols // col_tiles
    arrived = got_moments[holder].astype(jnp.float32).reshape(pair_count, 2, TILE, TILE)
    arrived_omega = got_omega[holder].astype(jnp.float32).reshape(pair_count, 2, TILE, TILE)
    gradient = (jnp.swapaxes(arrived[:, 0], 1, 2) + arrived[:, 1]) * 0.5
    on_diagonal = mine_rows[0::2] == mine_cols[0::2]
    identity = jnp.eye(TILE, dtype=jnp.float32)
    diag_mask = identity[None] * on_diagonal.astype(jnp.float32)[:, None, None]
    upper_omega = arrived_omega[:, 0]
    lower_omega = arrived_omega[:, 1]
    diag_values = jnp.sum(upper_omega * identity[None], axis=2)
    inverse = 1.0 / jnp.where(on_diagonal[:, None], diag_values, 1.0)
    gradient = gradient - diag_mask * inverse[:, :, None]
    scale = step[0]
    weight = 0.3 * jnp.exp(-0.12 * penalty[0].astype(jnp.float32))
    bound = scale * weight * (1.0 - diag_mask)
    upper_value = upper_omega - scale * gradient
    lower_value = lower_omega - scale * jnp.swapaxes(gradient, 1, 2)
    new_upper = upper_value - jnp.clip(upper_value, -bound, bound)
    new_lower = lower_value - jnp.clip(lower_value, -bound, bound)
    return (new_upper, new_lower)


def solution(mesh):
    placed = (P("row", "col"), P(None, "col"), P(), P(), P())
    return jax.shard_map(
        local,
        mesh=mesh,
        in_specs=placed,
        out_specs=(P(("row", "col"), None, None), P(("row", "col"), None, None)),
        check_vma=False,
    )
```

profile of v0, /device:TPU:0, one launch (start us, length us, event | category | flops | bytes accessed | tf_op | source)
XLA Modules:
  0.0 304.9 jit_solution(13373841002969201672)
XLA Ops:
  7.2 1.5 copy-done
  8.8 14.5 %fusion.24 = f32[4096,512]{1,0:T(8,128)} fusion(bf16[4096,2048]{1,0:T(8,128)(2,1)} %param.5, bf16[512,2048]{1,0:T(8,128)(2,1)S(1)} %copy-done), kind=kOutput, calls=%fused_computation.72 | convolution fusion | flops 8589934592 | bytes 27262976 | tf_op jit(solution)/shard_map/dot_general | solution.py:18
  23.3 0.2 all-gather.2.cloned.1.call-start
  23.5 92.2 %reduce-scatter.2.cloned.1.call-done = f32[512,512]{1,0:T(8,128)} async-done(((f32[4096,512]{1,0:T(8,128)}), f32[512,512]{1,0:T(8,128)}) %reduce-scatter.2.cloned.1.call-update) | async-done | bytes 1048592 | tf_op jit(solution)/shard_map/reduce_scatter | solution.py:21
  115.7 2.1 convert_element_type.46
  118.2 0.1 reduce_sum.70
  118.3 0.1 reduce_sum.66
  118.6 0.1 reduce_sum.48
  118.7 10.0 %copy.30 = bf16[512,8,16,128]{3,2,1,0:T(8,128)(2,1)S(1)} copy(bf16[512,8,16,128]{3,1,2,0:T(8,128)(2,1)} %bitcast.106) | data formatting | bytes 33554432
  128.7 8.2 %copy.19 = bf16[32,128,16,128]{3,1,2,0:T(8,128)(2,1)} copy(bf16[32,128,16,128]{3,2,1,0:T(8,128)(2,1)S(1)} %bitcast.105) | data formatting | bytes 33554432 | tf_op jit(solution)/shard_map/reshape | solution.py:48
  136.9 6.7 %gather_fusion = bf16[32,128,128]{2,1,0:T(8,128)(2,1)S(1)} fusion(bf16[32,128,16,128]{3,1,2,0:T(8,128)(2,1)} %copy.19, s32[32]{0:T(128)S(1)} %get-tuple-element.15), kind=kCustom, calls=%fused_computation | custom fusion | bytes 2097408 | tf_op jit(solution)/shard_map/gather | solution.py:48
  143.6 19.6 %all-gather.2.cloned.1.call-done = bf16[4096,512]{1,0:T(8,128)(2,1)} async-done(((bf16[512,512]{1,0:T(8,128)(2,1)}), bf16[4096,512]{1,0:T(8,128)(2,1)}) %all-gather.2.cloned.1.call-update) | async-done | bytes 4194320 | tf_op jit(solution)/shard_map/all_gather | solution.py:26
  163.3 14.6 %fusion = bf16[512,8,16,128]{3,1,2,0:T(8,128)(2,1)} fusion(bf16[4096,512]{1,0:T(8,128)(2,1)} %all-gather.2.cloned.1.call-done, bf16[512,2048]{1,0:T(8,128)(2,1)S(1)} %copy-done), kind=kOutput, calls=%fused_computation.5 | convolution fusion | flops 8606711808 | bytes 23068672 | tf_op jit(solution)/shard_map/dot_general | solution.py:24
  177.8 15.1 %copy.31 = bf16[512,8,16,128]{3,2,1,0:T(8,128)(2,1)} copy(bf16[512,8,16,128]{3,1,2,0:T(8,128)(2,1)} %fusion) | data formatting | bytes 33554432
  192.9 22.4 %copy.23 = bf16[16,128,32,128]{3,1,2,0:T(8,128)(2,1)} copy(bf16[16,128,32,128]{1,0,3,2:T(8,128)(2,1)} %bitcast.104) | data formatting | bytes 33554432 | tf_op jit(solution)/shard_map/reshape | solution.py:47
  215.3 6.5 %gather_fusion.2 = bf16[32,128,128]{2,1,0:T(8,128)(2,1)S(1)} fusion(bf16[16,128,32,128]{3,1,2,0:T(8,128)(2,1)} %copy.23, s32[32]{0:T(128)S(1)} %get-tuple-element.14), kind=kCustom, calls=%fused_computation.2 | custom fusion | bytes 2097408 | tf_op jit(solution)/shard_map/gather | solution.py:47
  221.8 1.2 broadcast_select_fusion
  223.0 30.8 %all_to_all.10 = bf16[32,128,128]{2,1,0:T(8,128)(2,1)} all-to-all(bf16[32,128,128]{2,1,0:T(8,128)(2,1)S(1)} %get-tuple-element.16), channel_id=1, replica_groups=mesh['row'=4,'col'=8] {'row','col'}, dimensions={0} | all-to-all | bytes 2097152 | tf_op jit(solution)/shard_map/all_to_all | solution.py:53
  253.8 3.4 %all-to-all-start = ((bf16[32,128,128]{2,1,0:T(8,128)(2,1)}), bf16[32,128,128]{2,1,0:T(8,128)(2,1)}, u32[]{:S(2)}, u32[]{:S(2)}) async-start(bf16[32,128,128]{2,1,0:T(8,128)(2,1)} %get-tuple-element.17), calls=%async_computation | async-start | bytes 2097152 | tf_op jit(solution)/shard_map/all_to_all | solution.py:54
  257.2 0.1 copy.20
  257.4 0.1 copy.21
  259.5 1.9 gather_fusion.3
  261.4 1.2 convert.2
  262.6 0.9 slice.44
  263.5 21.1 %all-to-all-done = bf16[32,128,128]{2,1,0:T(8,128)(2,1)} async-done(((bf16[32,128,128]{2,1,0:T(8,128)(2,1)}), bf16[32,128,128]{2,1,0:T(8,128)(2,1)}, u32[]{:S(2)}, u32[]{:S(2)}) %all-to-all-start) | async-done | bytes 1048608 | tf_op jit(solution)/shard_map/all_to_all | solution.py:54
  284.6 2.7 gather_fusion.1
  287.3 1.2 convert.3
  288.6 2.2 copy.28
  290.7 0.2 multiply_reduce_fusion
  291.0 2.7 fusion.21
  293.7 2.2 copy.26
  295.9 2.2 fusion.10
  (28 shorter events, 1.1 us)
Async XLA Ops:
  7.2 1.6 copy-start
  7.2 108.5 %reduce-scatter.2.cloned.1.call-start = ((), (), s32[]{:S(2)}) async-start(), calls=%async_computation.3 | async-start | bytes 9437184 | tf_op jit(solution)/shard_map/reduce_scatter | solution.py:21
  23.3 94.7 %copy-start.2 = (s32[320,2]{0,1:T(2,128)S(1)}, s32[320,2]{0,1:T(2,128)}, u32[]{:S(2)}) copy-start(s32[320,2]{0,1:T(2,128)} %param.7) | copy-start | bytes 7684
  23.3 140.0 %all-gather.2.cloned.1.call-start = ((), (), s32[]{:S(2)}) async-start(), calls=%async_computation.4 | async-start | bytes 4718592 | tf_op jit(solution)/shard_map/all_gather | solution.py:26
  253.8 30.8 %all-to-all-start = ((bf16[32,128,128]{2,1,0:T(8,128)(2,1)}), bf16[32,128,128]{2,1,0:T(8,128)(2,1)}, u32[]{:S(2)}, u32[]{:S(2)}) async-start(bf16[32,128,128]{2,1,0:T(8,128)(2,1)} %get-tuple-element.17), calls=%async_computation | async-start | bytes 2097152 | tf_op jit(solution)/shard_map/all_to_all | solution.py:54
  257.6 40.5 %copy-start.1 = (bf16[512,2048]{1,0:T(8,128)(2,1)S(1)}, bf16[512,2048]{1,0:T(8,128)(2,1)}, u32[]{:S(2)}) copy-start(bf16[512,2048]{1,0:T(8,128)(2,1)} %param.6) | copy-start | bytes 6291460
Sparse Core Ops, SparseCore 0:
  23.4 92.2 reduce-scatter.1
  117.9 45.3 all-gather.1
where the time goes:
time: 306 us; the launch traced here: 305 us
  waiting for transfers between devices  133 us (43%)
  local copies, waits for them, and re-layouts  81.4 us (27%)
  blocking collectives  30.8 us (10%)
  matrix products  29 us (9%)
  between operations  15.8 us (5%)
  other arithmetic  11.3 us (4%)
  starting transfers between devices  3.64 us (1%)
    reduce_scatter x1, waiting for transfers between devices, local(): lax.psum_scatter(partial_value, 'col', scatter_dimension=0, tiled=True)  92.2 us
    all_to_all x1, blocking collectives, local(): lax.all_to_all(send_moments, ('row', 'col'), split_axis=0, concat_axis=0,...  30.8 us
    unnamed x10, local copies, waits for them, and re-layouts  28.9 us
    reshape x1, local copies, waits for them, and re-layouts, local(): moments.reshape(col_tiles, TILE, row_tiles, TILE)  22.4 us
    all_to_all x1, waiting for transfers between devices, local(): lax.all_to_all(send_omega, ('row', 'col'), split_axis=0, concat_axis=0, t...  21.1 us
    all_gather x1, waiting for transfers between devices, local(): lax.all_gather(shared, 'col', axis=0, tiled=True)  19.6 us
    dot_general x1, matrix products, local(): lax.dot_general(samples, lax.all_gather(shared, 'col', axis=0, tiled=True...  14.6 us
    dot_general x1, matrix products, local(): lax.dot_general(omega, samples, (((1,), (1,)), ((), ())), preferred_eleme...  14.5 us
  transfers between devices with their start and end apart: 3, of which 3 were waited for; matrix products, arithmetic and copies ran while one was open for 10% of the time, Pallas kernels for 0%

commit v1 on v0

v1 whole, which is shorter than its diff:
```python
import functools

import jax
import jax.numpy as jnp
from jax import lax
from jax.experimental import pallas as pl
from jax.experimental.pallas import tpu as pltpu
from jax.sharding import Mesh, PartitionSpec as P

TILE = 128
ANY = pl.BlockSpec(memory_space=pl.ANY)
SMEM = pl.BlockSpec(memory_space=pltpu.SMEM)
VMEM = pl.BlockSpec(memory_space=pltpu.VMEM)
AXES = ("row", "chip", "core")


def tile_at(index):
    return pl.ds(pl.multiple_of(index * TILE, TILE), TILE)


def pick_kernel(rows, cols, omega, out, sems):
    count = out.shape[0]

    def copy(i):
        return pltpu.make_async_copy(
            omega.at[tile_at(rows[i]), tile_at(cols[i])], out.at[i], sems.at[i]
        )

    def start(i, carry):
        copy(i).start()
        return carry

    def wait(i, carry):
        copy(i).wait()
        return carry

    lax.fori_loop(0, count, start, 0)
    lax.fori_loop(0, count, wait, 0)


def pick_tiles(omega, rows, cols):
    count = rows.shape[0]
    return pl.pallas_call(
        pick_kernel,
        out_shape=jax.ShapeDtypeStruct((count, TILE, TILE), omega.dtype),
        in_specs=[SMEM, SMEM, ANY],
        out_specs=VMEM,
        scratch_shapes=[pltpu.SemaphoreType.DMA((count,))],
        name="pick_tiles",
    )(rows, cols, omega)


def moment_kernel(samples_scale, rows, cols, info, shared, own, other, out):
    count = out.shape[0]
    core, diagonal = info[0], info[1]
    half = own.shape[1] // TILE

    def product(row, col, write):
        def from_block(block):
            value = jnp.dot(
                shared[tile_at(row), :],
                block[:, tile_at(lax.rem(col, half))],
                preferred_element_type=jnp.float32,
            )
            write((value * samples_scale).astype(jnp.bfloat16))

        pl.when(col // half == core)(lambda: from_block(own))
        pl.when(col // half != core)(lambda: from_block(other))

    def step(i, carry):
        def write(value):
            out[i] = value

        product(rows[i], cols[i], write)
        return carry

    def merge(i, carry):
        def write(value):
            partner = value.astype(jnp.float32).T
            out[i] = ((out[i].astype(jnp.float32) + partner) * 0.5).astype(jnp.bfloat16)

        product(cols[i], rows[i], write)
        return carry

    lax.fori_loop(0, count, step, 0)

    @pl.when(diagonal == 1)
    def _():
        lax.fori_loop(0, count, merge, 0)


def moment_tiles(shared, own, other, rows, cols, info):
    count = rows.shape[0]
    depth = shared.shape[1]
    return pl.pallas_call(
        functools.partial(moment_kernel, 1.0 / depth),
        out_shape=jax.ShapeDtypeStruct((count, TILE, TILE), jnp.bfloat16),
        in_specs=[SMEM, SMEM, SMEM, VMEM, VMEM, VMEM],
        out_specs=VMEM,
        compiler_params=pltpu.CompilerParams(vmem_limit_bytes=32 * 1024 * 1024),
        name="moment_tiles",
    )(rows, cols, info, shared, own, other)


def update_kernel(
    table, scalars, mine_up, mine_low, omega_up, omega_low, new_upper, new_lower
):
    k = pl.program_id(0)
    merged, equal = table[4, k], table[5, k]
    scale, weight = scalars[0], scalars[1]
    up = mine_up[0].astype(jnp.float32)
    low = mine_low[0].astype(jnp.float32).T
    gradient = jnp.where(merged == 1, up, (up + low) * 0.5)
    upper = omega_up[0].astype(jnp.float32)
    lower = omega_low[0].astype(jnp.float32)
    row = lax.broadcasted_iota(jnp.int32, (TILE, TILE), 0)
    col = lax.broadcasted_iota(jnp.int32, (TILE, TILE), 1)
    diagonal = (row == col) & (equal == 1)
    gradient = gradient - jnp.where(diagonal, 1.0 / jnp.where(diagonal, upper, 1.0), 0.0)
    bound = jnp.where(diagonal, 0.0, scale * weight)
    upper_value = upper - scale * gradient
    lower_value = lower - scale * gradient.T
    new_upper[0] = upper_value - jnp.clip(upper_value, -bound, bound)
    new_lower[0] = lower_value - jnp.clip(lower_value, -bound, bound)


def update(got_moments, got_omega, table, scalars):
    count = table.shape[1]
    tile = (1, TILE, TILE)

    def slot(line):
        return pl.BlockSpec(tile, lambda k, table, scalars: (table[line, k], 0, 0))

    out = pl.BlockSpec(tile, lambda k, table, scalars: (k, 0, 0))
    shape = jax.ShapeDtypeStruct((count, TILE, TILE), jnp.float32)
    return pl.pallas_call(
        update_kernel,
        out_shape=(shape, shape),
        grid_spec=pltpu.PrefetchScalarGridSpec(
            num_scalar_prefetch=2,
            grid=(count,),
            in_specs=[slot(0), slot(1), slot(2), slot(3)],
            out_specs=[out, out],
        ),
        name="update",
    )(table, scalars, got_moments, got_moments, got_omega, got_omega)


def local(omega, samples, pair_tiles, step, penalty):
    rows, chips, cores = (lax.axis_size(name) for name in AXES)
    row, chip, core = (lax.axis_index(name) for name in AXES)
    own_index = (row * chips + chip) * cores + core
    row_tiles = omega.shape[0] // TILE
    col_tiles = omega.shape[1] // TILE
    devices = rows * chips * cores
    pair_count = pair_tiles.shape[0] // devices
    other = lax.ppermute(samples, "core", [(i, cores - 1 - i) for i in range(cores)])

    pairs = pair_tiles.reshape(devices, pair_count, 2)
    first, second = pairs[:, :, 0], pairs[:, :, 1]
    wanted = (first // row_tiles == jnp.minimum(row, chip)) & (
        second // row_tiles == jnp.maximum(row, chip)
    )
    wanted = wanted.astype(jnp.int32)
    upper = jnp.sum(wanted * first, axis=1)
    lower = jnp.sum(wanted * second, axis=1)
    flip = row > chip
    tile_row = jnp.where(flip, lower, upper) - row * row_tiles
    tile_col = jnp.where(flip, upper, lower) - chip * row_tiles
    mine = lambda x: lax.dynamic_index_in_dim(
        x.reshape(rows * chips, cores), core, 1, keepdims=False
    )
    held = tile_col // col_tiles == core
    use_swapped = (row == chip) & ~held
    omega_row = jnp.where(use_swapped, tile_col, tile_row)
    omega_col = jnp.where(use_swapped, tile_row, tile_col) % col_tiles
    sent_omega = pick_tiles(omega, omega_row, omega_col)
    got_omega = lax.all_to_all(sent_omega, AXES, split_axis=0, concat_axis=0, tiled=True)

    partial_value = lax.dot_general(
        omega, samples, (((1,), (1,)), ((), ())), preferred_element_type=jnp.float32
    )
    scattered = lax.psum_scatter(
        partial_value, ("chip", "core"), scatter_dimension=0, tiled=True
    ).astype(jnp.bfloat16)
    shared = lax.all_gather(scattered, ("chip", "core"), axis=0, tiled=True)
    info = jnp.stack([core, (row == chip).astype(jnp.int32)])
    sent_moments = moment_tiles(
        shared,
        samples,
        other,
        mine(tile_row),
        mine(tile_col),
        info,
    )
    got_moments = lax.all_to_all(
        sent_moments, ("row", "chip"), split_axis=0, concat_axis=0, tiled=True
    )

    mine_pairs = lax.dynamic_index_in_dim(pairs, own_index, 0, keepdims=False)
    one, two = mine_pairs[:, 0], mine_pairs[:, 1]
    one_block, two_block = one // row_tiles, two // row_tiles
    table = jnp.stack(
        [
            one_block * chips + two_block,
            two_block * chips + one_block,
            one_block * chips * cores + two // col_tiles,
            two_block * chips * cores + one // col_tiles,
            (one_block == two_block).astype(jnp.int32),
            (one == two).astype(jnp.int32),
        ]
    )
    weight = 0.3 * jnp.exp(-0.12 * penalty.astype(jnp.float32))
    scalars = jnp.concatenate([step, weight])
    return update(got_moments, got_omega, table, scalars)


def solution(mesh):
    rows, cols = mesh.shape["row"], mesh.shape["col"]
    cores = cols // rows
    view = Mesh(mesh.devices.reshape(rows, rows, cores), AXES)
    placed = (P("row", ("chip", "core")), P(None, ("chip", "core")), P(), P(), P())
    out = P(AXES, None, None)
    return jax.shard_map(
        local, mesh=view, in_specs=placed, out_specs=(out, out), check_vma=False
    )
```

time: 306 us -> 235 us (0.77)
  local copies, waits for them, and re-layouts: 81.4 us -> 4.08 us
  waiting for transfers between devices: 133 us -> 166 us
  blocking collectives: 30.8 us -> 0 us
  Pallas kernels: 0 us -> 20.9 us
  matrix products: 29 us -> 15.1 us
  other arithmetic: 11.3 us -> 4.1 us
  starting transfers between devices: 3.64 us -> 7.59 us
    all_gather x1, waiting for transfers between devices: 19.6 us -> 59.6 us  [local(): shared = lax.all_gather(scattered, ('chip', 'core'), axis=0, tiled=True)]
    all_to_all x1 -> x0, blocking collectives: 30.8 us -> none  [local(): lax.all_to_all(send_moments, ('row', 'col'), split_axis=0, concat_axis=0,...]
    reshape x4 -> x1, local copies, waits for them, and re-layouts: 30.8 us -> 0.1 us  [local(): pairs = pair_tiles.reshape(devices, pair_count, 2)]
    unnamed x10, local copies, waits for them, and re-layouts: 28.9 us -> 3 us
    pallas_call x0 -> x3, Pallas kernels: none -> 20.9 us  [the longest x1 10.4 us: moment_tiles(): pl.pallas_call(functools.partial(moment_kernel, 1.0 / depth), out_shape=j...]
    gather x4 -> x0, local copies, waits for them, and re-layouts: 17.8 us -> none  [the longest x1 6.7 us: local(): omega.reshape(row_tiles, TILE, col_tiles, TILE)]
    dot_general x1 -> x0, matrix products: 14.6 us -> none  [local(): lax.dot_general(samples, lax.all_gather(shared, 'col', axis=0, tiled=True...]
    all_to_all x1 -> x2, waiting for transfers between devices: 21.1 us -> 14 us  [the longest x1 14 us: local(): lax.all_to_all(sent_moments, ('row', 'chip'), split_axis=0, concat_axis=0...]
  transfers between devices with their start and end apart: 3 -> 5, of which waited for: 3 -> 3; matrix products, arithmetic and copies ran while one was open for 10% -> 1% of each run, Pallas kernels for 0% -> 6%
where the time goes in v1:
time: 235 us; the launch traced here: 233 us
  waiting for transfers between devices  166 us (71%)
  Pallas kernels  20.9 us (9%)
  between operations  15.5 us (7%)
  matrix products  15.1 us (6%)
  starting transfers between devices  7.59 us (3%)
  other arithmetic  4.1 us (2%)
  local copies, waits for them, and re-layouts  4.08 us (2%)
    reduce_scatter x1, waiting for transfers between devices, local(): lax.psum_scatter(partial_value, ('chip', 'core'), scatter_dimension=0, ti...  92.3 us
    all_gather x1, waiting for transfers between devices, local(): shared = lax.all_gather(scattered, ('chip', 'core'), axis=0, tiled=True)  59.6 us
    dot_general x1, matrix products, local(): lax.dot_general(omega, samples, (((1,), (1,)), ((), ())), preferred_eleme...  15.1 us
    all_to_all x1, waiting for transfers between devices, local(): lax.all_to_all(sent_moments, ('row', 'chip'), split_axis=0, concat_axis=0...  14 us
    pallas_call x1, Pallas kernels, moment_tiles(): pl.pallas_call(functools.partial(moment_kernel, 1.0 / depth), out_shape=j...  10.4 us
    pallas_call x1, Pallas kernels, update(): pl.pallas_call(update_kernel, out_shape=(shape, shape), grid_spec=pltpu.P...  7.25 us
  transfers between devices with their start and end apart: 5, of which 3 were waited for; matrix products, arithmetic and copies ran while one was open for 1% of the time, Pallas kernels for 6%

profile of v1, /device:TPU:0, one launch (start us, length us, event | category | flops | bytes accessed | tf_op | source)
XLA Modules:
  0.0 233.3 jit_solution(12435204226983984202)
XLA Ops:
  7.2 0.0 reduce-scatter.2.cloned.1.call-start
  7.2 15.1 %fusion.14 = f32[4096,512]{1,0:T(8,128)} fusion(bf16[4096,2048]{1,0:T(8,128)(2,1)} %omega.1, bf16[512,2048]{1,0:T(8,128)(2,1)} %own.1), kind=kOutput, calls=%fused_computation.61 | convolution fusion | flops 8589934592 | bytes 27262976 | tf_op jit(solution)/shard_map/dot_general | solution.py:180
  22.3 0.0 reduce-scatter.2.cloned.1.call-update
  22.3 0.0 all-gather.2.cloned.1.call-start
  22.4 92.3 %reduce-scatter.2.cloned.1.call-done = f32[512,512]{1,0:T(8,128)} async-done(((f32[4096,512]{1,0:T(8,128)}), f32[512,512]{1,0:T(8,128)}) %reduce-scatter.2.cloned.1.call-update) | async-done | bytes 1048592 | tf_op jit(solution)/shard_map/reduce_scatter | solution.py:183
  114.7 2.1 convert_element_type.31
  116.8 0.0 all-gather.2.cloned.1.call-update
  116.8 0.0 copy-done.1
  116.9 0.1 collective-permute-start
  117.0 0.0 copy-done.4
  117.0 0.1 reshape.375
  117.1 0.1 select_reduce_fusion
  117.2 0.6 and_select_fusion
  117.8 0.6 select_n.129.rows
  118.4 3.2 %pick_tiles.1 = bf16[32,128,128]{2,1,0:T(8,128)(2,1)} custom-call(s32[32]{0:T(128)} %select_n.129.rows, s32[32]{0:T(128)} %get-tuple-element.4.cols, bf16[4096,2048]{1,0:T(8,128)(2,1)} %omega.1), custom_call_target="tpu_custom_call" | custom-call | tf_op jit(solution)/shard_map/pick_tiles/pallas_call | solution.py:43
  121.6 3.2 %all-to-all-start.1 = ((bf16[32,128,128]{2,1,0:T(8,128)(2,1)}), bf16[32,128,128]{2,1,0:T(8,128)(2,1)S(1)}, u32[]{:S(2)}, u32[]{:S(2)}) async-start(bf16[32,128,128]{2,1,0:T(8,128)(2,1)} %pick_tiles.1), calls=%async_computation.2 | async-start | bytes 2097152 | tf_op jit(solution)/shard_map/all_to_all | solution.py:178
  124.7 0.1 sub.60
  124.8 0.1 sub.57
  124.9 0.2 dynamic-slice_reduce_fusion
  125.1 0.1 pad_add_fusion.info
  125.2 0.0 collective-permute-done.other
  125.2 59.6 %all-gather.2.cloned.1.call-done.shared = bf16[4096,512]{1,0:T(8,128)(2,1)} async-done(((bf16[512,512]{1,0:T(8,128)(2,1)}), bf16[4096,512]{1,0:T(8,128)(2,1)}) %all-gather.2.cloned.1.call-update) | async-done | bytes 4194320 | tf_op jit(solution)/shard_map/all_gather | solution.py:186
  184.8 2.2 copy-done
  187.0 10.4 %moment_tiles.1 = bf16[16,128,128]{2,1,0:T(8,128)(2,1)} custom-call(s32[16]{0:T(128)S(1)} %get-tuple-element.17.rows, s32[16]{0:T(128)S(1)} %get-tuple-element.16.cols, s32[2]{0:T(128)S(1)} %pad_add_fusion.info, bf16[4096,512]{1,0:T(8,128)(2,1)S(1)} %copy-done, bf16[512,2048]{1,0:T(8,128)(2,1)S(1)} %copy-done.1, bf16[512,2048]{1,0:T(8,128)(2,1)} %collective-permute-done.other), custom_call_target="tpu_custom_call" | custom-call | tf_op jit(solution)/shard_map/moment_tiles/pallas_call | solution.py:95
  197.4 0.0 all-to-all-done.1.omega_up.omega_low
  197.5 4.3 %all-to-all-start = ((bf16[16,128,128]{2,1,0:T(8,128)(2,1)}), bf16[16,128,128]{2,1,0:T(8,128)(2,1)S(1)}, u32[]{:S(2)}, u32[]{:S(2)}) async-start(bf16[16,128,128]{2,1,0:T(8,128)(2,1)} %moment_tiles.1), calls=%async_computation.1 | async-start | bytes 1048576 | tf_op jit(solution)/shard_map/all_to_all | solution.py:196
  203.2 0.6 stack.21.table
  203.8 0.6 pad_maximum_fusion.scalars
  204.4 14.0 %all-to-all-done.mine_up.mine_low = bf16[16,128,128]{2,1,0:T(8,128)(2,1)S(1)} async-done(((bf16[16,128,128]{2,1,0:T(8,128)(2,1)}), bf16[16,128,128]{2,1,0:T(8,128)(2,1)S(1)}, u32[]{:S(2)}, u32[]{:S(2)}) %all-to-all-start) | async-done | bytes 524320 | tf_op jit(solution)/shard_map/all_to_all | solution.py:196
  218.4 0.0 copy-done.2
  218.4 0.8 copy-done.3
  219.2 7.2 %update.1 = (f32[10,128,128]{2,1,0:T(8,128)}, f32[10,128,128]{2,1,0:T(8,128)}) custom-call(s32[6,10]{1,0:T(8,128)} %stack.21.table, f32[2]{0:T(128)} %pad_maximum_fusion.scalars, bf16[16,128,128]{2,1,0:T(8,128)(2,1)} %copy-done.3, bf16[16,128,128]{2,1,0:T(8,128)(2,1)} %copy-done.3, bf16[32,128,128]{2,1,0:T(8,128)(2,1)} %copy-done.2, ...), custom_call_target="tpu_custom_call" | custom-call | tf_op jit(solution)/shard_map/update/pallas_call | solution.py:136
  (8 shorter events, 0.0 us)
Async XLA Ops:
  7.2 107.6 %reduce-scatter.2.cloned.1.call-start = ((), (), s32[]{:S(2)}) async-start(), calls=%async_computation.3 | async-start | bytes 9437184 | tf_op jit(solution)/shard_map/reduce_scatter | solution.py:183
  22.3 94.5 %copy-start.1 = (bf16[512,2048]{1,0:T(8,128)(2,1)S(1)}, bf16[512,2048]{1,0:T(8,128)(2,1)}, u32[]{:S(2)}) copy-start(bf16[512,2048]{1,0:T(8,128)(2,1)} %own.1) | copy-start | bytes 6291460
  22.3 94.6 %copy-start.4 = (s32[320,2]{0,1:T(2,128)S(1)}, s32[320,2]{0,1:T(2,128)}, u32[]{:S(2)}) copy-start(s32[320,2]{0,1:T(2,128)} %param.7) | copy-start | bytes 7684
  22.3 162.5 %all-gather.2.cloned.1.call-start = ((), (), s32[]{:S(2)}) async-start(), calls=%async_computation.4 | async-start | bytes 4718592 | tf_op jit(solution)/shard_map/all_gather | solution.py:186
  116.9 8.3 %collective-permute-start = (bf16[512,2048]{1,0:T(8,128)(2,1)S(1)}, bf16[512,2048]{1,0:T(8,128)(2,1)}, u32[]{:S(2)}, u32[]{:S(2)}) collective-permute-start(bf16[512,2048]{1,0:T(8,128)(2,1)S(1)} %copy-done.1), channel_id=1, source_target_pairs={{0,1},{1,0},{2,3},{3,2},{4,5},{5,4},{6,7},{7,6},{8,9},{9,8},{10,11... | collective-permute-start | bytes 6291464 | tf_op jit(solution)/shard_map/ppermute | solution.py:157
  121.6 75.9 %all-to-all-start.1 = ((bf16[32,128,128]{2,1,0:T(8,128)(2,1)}), bf16[32,128,128]{2,1,0:T(8,128)(2,1)S(1)}, u32[]{:S(2)}, u32[]{:S(2)}) async-start(bf16[32,128,128]{2,1,0:T(8,128)(2,1)} %pick_tiles.1), calls=%async_computation.2 | async-start | bytes 2097152 | tf_op jit(solution)/shard_map/all_to_all | solution.py:178
  184.8 2.2 copy-start
  197.4 20.9 %copy-start.2 = (bf16[32,128,128]{2,1,0:T(8,128)(2,1)}, bf16[32,128,128]{2,1,0:T(8,128)(2,1)S(1)}, u32[]{:S(2)}) copy-start(bf16[32,128,128]{2,1,0:T(8,128)(2,1)S(1)} %all-to-all-done.1.omega_up.omega_low) | copy-start | bytes 3145732
  197.5 20.9 %all-to-all-start = ((bf16[16,128,128]{2,1,0:T(8,128)(2,1)}), bf16[16,128,128]{2,1,0:T(8,128)(2,1)S(1)}, u32[]{:S(2)}, u32[]{:S(2)}) async-start(bf16[16,128,128]{2,1,0:T(8,128)(2,1)} %moment_tiles.1), calls=%async_computation.1 | async-start | bytes 1048576 | tf_op jit(solution)/shard_map/all_to_all | solution.py:196
  218.4 0.8 copy-start.3
Sparse Core Ops, SparseCore 0:
  22.5 92.2 reduce-scatter.1
  117.0 67.7 all-gather.1
